TPU v7x, 512 devices: a whole 4x8x8 slice. The times are simulated.
512 devices in a mesh: area: 8 (over y), hor: 16 (over z, core), scen: 4 (over x).
Axes of the slice: x: 4, y: 8, z: 8, core: 2. Of those that a mesh axis runs over, the one named last changes fastest.
Arguments:
- diagonal: float32 [8, 32, 384], P('area', 'hor'), may hold values from 0.25 to 1
- band_coef: float32 [8, 32, 4, 384], P('area', 'hor'), may hold values from -0.1 to 0.1
- band_offsets: int32 [8, 4], P('area'), may hold values from -16 to 16, as said below
- boundary_index: int32 [8, 128], P('area'), may hold values from 0 to 383, as said below
- adjacency: int32 [8, 3], P('area'), may hold values from 0 to 7, as said below
- start_state: float32 [8, 384], P('area'), may hold values from -6 to 6
- input_matrix: float32 [8, 384, 128], P('area'), may hold values from -0.3125 to 0.3125
- input_penalty: float32 [8, 128], P('area'), may hold values from 0.5 to 2
- linear_cost: float32 [8, 32, 64, 384], P('area', 'hor', 'scen'), may hold values from -1.2 to 1.2
- disturbance: float32 [8, 32, 64, 384], P('area', 'hor', 'scen'), may hold values from -0.6 to 0.6
- consensus: float32 [8, 32, 64, 128], P('area', 'hor', 'scen'), may hold values from -1.8 to 1.8
- dual_values: float32 [8, 32, 64, 128], P('area', 'hor', 'scen'), may hold values from -1.8 to 1.8
Outputs:
- trajectory: float32 [8, 32, 64, 384], P('area', 'hor', 'scen')
- agreed_boundary: float32 [8, 32, 64, 128], P('area', 'hor', 'scen')
- updated_duals: float32 [8, 32, 64, 128], P('area', 'hor', 'scen')
Inputs may be any that keep to these rules, and one draw needn't show every extreme that they name: `band_offsets`: every entry is 16 or -16; the first two entries of every row are 16 and -16. `boundary_index`: the entries of a row are distinct, and every row holds 0 and 383. `adjacency`: the first entry of row a differs from a; the other entries may repeat and may equal a.
All inputs are finite; a program needn't handle non-finite values.
Results may differ from a plain program's by a relative error of at most 0.0003.
Values sent between devices are 32-bit elements; how exact they have to be, the bound alone decides.
A program may use at most 64 MiB of HBM per device.

v0:
```python
import jax
import jax.numpy as jnp
from jax import lax
from jax.sharding import PartitionSpec as P

MAXOFF = 16
NNB = 3


highest = lax.Precision.HIGHEST


def carried_in(shard, axis, combine, identity, reverse):
    devices, place = (lax.axis_size(axis), lax.axis_index(axis))
    everything = jax.tree.map(lambda part: lax.all_gather(part, axis), shard)
    start = jax.tree.map(
        lambda part, zero: jnp.broadcast_to(jnp.asarray(zero, part.dtype), part.shape),
        shard,
        identity,
    )

    def lap(k, before):
        at = devices - 1 - k if reverse else k
        reached = at > place if reverse else at < place
        new = combine(before, jax.tree.map(lambda part: part[at], everything))
        return jax.tree.map(lambda a, b: jnp.where(reached, a, b), new, before)

    return lax.fori_loop(0, devices, lap, start)


def sent_to_all(shard, axis):
    copies = jnp.broadcast_to(shard, (lax.axis_size(axis), *shard.shape))
    return lax.all_to_all(copies, axis, split_axis=0, concat_axis=0, tiled=True)


def over_copies(shard, axis):
    return sent_to_all(shard, axis).sum(axis=0)


def laid_out(tiles, dim):
    tiles = jnp.moveaxis(tiles, 0, dim)
    lengths = tiles.shape
    return tiles.reshape(*lengths[:dim], lengths[dim] * lengths[dim + 1], *lengths[dim + 2 :])


def collect(shard, axis, dim):
    tiles = sent_to_all(shard, axis)
    return laid_out(tiles, dim)


def shifted(values, offset):
    extent = values.shape[-1]
    padding = [(0, 0)] * (values.ndim - 1) + [(MAXOFF, MAXOFF)]
    padded = jnp.pad(values, padding)
    return lax.dynamic_slice_in_dim(padded, MAXOFF + offset, extent, values.ndim - 1)


def forward_apply(values, diag_row, band_rows, offsets):
    result = diag_row * values
    for band_index in range(band_rows.shape[0]):
        result = result + band_rows[band_index] * shifted(values, offsets[band_index])
    return result


def backward_apply(values, diag_row, band_rows, offsets):
    result = diag_row * values
    for band_index in range(band_rows.shape[0]):
        result = result + shifted(band_rows[band_index] * values, -offsets[band_index])
    return result


def product(left, right):
    return jnp.dot(left, right, precision=highest, preferred_element_type=jnp.float32)


def product_transposed(left, right):
    return lax.dot_general(
        left, right, (((1,), (1,)), ((), ())), precision=highest, preferred_element_type=jnp.float32
    )


def per_device(
    diagonal,
    band_coef,
    band_offsets,
    boundary_index,
    adjacency,
    start_state,
    input_matrix,
    input_penalty,
    linear_cost,
    disturbance,
    consensus,
    dual_values,
):
    diagonals = diagonal[0]
    band_rows = band_coef[0]
    offsets = band_offsets[0]
    matrix = input_matrix[0]
    section_count = diagonals.shape[0]
    states_count = diagonals.shape[1]
    selection = (jnp.arange(states_count)[:, None] == boundary_index[0][None, :]).astype(
        jnp.float32
    )
    gradient = linear_cost[0] + jnp.einsum(
        "tsk,ik->tsi", dual_values[0] - consensus[0], selection, precision=highest
    )
    identity = jnp.eye(states_count, dtype=jnp.float32)
    segment = identity
    for section_index in reversed(range(section_count)):
        segment = backward_apply(
            segment, diagonals[section_index], band_rows[section_index], offsets
        )
    zero_rows = jnp.zeros(gradient.shape[1:], jnp.float32)
    local_costate = zero_rows
    for section_index in reversed(range(section_count)):
        local_costate = (
            backward_apply(
                local_costate, diagonals[section_index], band_rows[section_index], offsets
            )
            + gradient[section_index]
        )
    position = lax.axis_index("hor")

    def join_back(earlier, later_part):
        return (
            product(earlier[0], later_part[0]),
            product(earlier[1], later_part[0]) + later_part[1],
        )

    composite = carried_in((segment, local_costate), "hor", join_back, (identity, zero_rows), True)
    costate_end = composite[1]
    after_list = [None] * section_count
    running = costate_end
    for section_index in reversed(range(section_count)):
        after_list[section_index] = running
        if section_index > 0:
            running = (
                backward_apply(running, diagonals[section_index], band_rows[section_index], offsets)
                + gradient[section_index]
            )
    costate_after = jnp.stack(after_list)
    controls = (
        -jnp.einsum("tsi,iu->tsu", costate_after, matrix, precision=highest) / input_penalty[0]
    )
    first_total = over_copies(jnp.sum(controls[0], axis=0), "scen")
    scenario_total = controls.shape[1] * lax.axis_size("scen")
    shared_first = jnp.broadcast_to(first_total / scenario_total, controls[0].shape)
    first_row = jnp.where(position == 0, shared_first, controls[0])
    controls = jnp.concatenate([first_row[None], controls[1:]], axis=0)
    forcing = jnp.einsum("tsu,iu->tsi", controls, matrix, precision=highest) + disturbance[0]
    local_state = zero_rows
    for section_index in range(section_count):
        local_state = (
            forward_apply(local_state, diagonals[section_index], band_rows[section_index], offsets)
            + forcing[section_index]
        )
    initial = jnp.broadcast_to(start_state[0], zero_rows.shape)

    def join_ahead(earlier, later_part):
        return (
            product(later_part[0], earlier[0]),
            product_transposed(earlier[1], later_part[0]) + later_part[1],
        )

    composite = carried_in((segment, local_state), "hor", join_ahead, (identity, zero_rows), False)
    state_begin = product_transposed(initial, composite[0]) + composite[1]
    states_list = []
    running = state_begin
    for section_index in range(section_count):
        states_list.append(running)
        if section_index + 1 < section_count:
            running = (
                forward_apply(running, diagonals[section_index], band_rows[section_index], offsets)
                + forcing[section_index]
            )
    trajectory = jnp.stack(states_list)
    boundary = jnp.einsum("tsi,ik->tsk", trajectory, selection, precision=highest)
    own_area = lax.axis_index("area")
    neighbours = adjacency[0]
    arrived_rows = collect(boundary[None], "area", 0)
    area_ids = jnp.arange(arrived_rows.shape[0], dtype=jnp.int32)
    weights = (area_ids == own_area).astype(jnp.float32)
    weights = weights + jnp.sum(
        (neighbours[:, None] == area_ids[None, :]).astype(jnp.float32), axis=0
    )
    summed = jnp.zeros_like(boundary) + jnp.einsum(
        "n,ntsk->tsk", weights, arrived_rows, precision=highest
    )
    agreed = summed / (NNB + 1)
    updated = dual_values[0] + boundary - agreed
    return (trajectory[None], agreed[None], updated[None])


def solution(mesh):
    in_specs = (
        P("area", "hor", None),
        P("area", "hor", None, None),
        P("area", None),
        P("area", None),
        P("area", None),
        P("area", None),
        P("area", None, None),
        P("area", None),
        P("area", "hor", "scen", None),
        P("area", "hor", "scen", None),
        P("area", "hor", "scen", None),
        P("area", "hor", "scen", None),
    )
    out_specs = (
        P("area", "hor", "scen", None),
        P("area", "hor", "scen", None),
        P("area", "hor", "scen", None),
    )
    return jax.shard_map(
        per_device, mesh=mesh, in_specs=in_specs, out_specs=out_specs, check_vma=False
    )
```

profile of v0, /device:TPU:1, one launch (start us, length us, event | category | flops | bytes accessed | tf_op | source)
XLA Modules:
  0.0 229.5 jit_solution(6935506005120938105)
XLA Ops:
  21.6 26.7 %all-gather.1 = f32[256,384]{1,0:T(8,128)S(1)} all-gather(f32[16,384]{1,0:T(8,128)S(1)} %fusion.54), channel_id=3, replica_groups=mesh['area'=8,'hor'=16,'scen'=4] {'hor'}, dimensions={0}, use_global_device_ids=true | all-gather | bytes 417792 | tf_op jit(solution)/shard_map/all_gather | solution.py:15
  48.3 38.4 %all-gather.5.cloned.1.call-done = f32[6144,384]{1,0:T(8,128)} async-done(((f32[384,384]{1,0:T(8,128)}), f32[6144,384]{1,0:T(8,128)}) %all-gather.5.cloned.1.call-update) | async-done | bytes 9437200 | tf_op jit(solution)/shard_map/all_gather | solution.py:15
  86.7 24.8 %while.32 = (s32[]{:T(128)}, f32[16,384]{1,0:T(8,128)S(1)}, s32[]{:T(128)}, f32[16,384,384]{2,1,0:T(8,128)}, f32[16,16,384]{2,1,0:T(8,128)S(1)}, /*index=5*/s32[]{:T(128)}, s32[]{:T(128)}, s32[]{:T(128)}, s32[]{:T(128)}) while((s32[]{:T(128)}, f32[16,384]{1,0:T(8,128)S(1)}, s32[]{:T(128)}, f32[16,384,384]{2,1,0:T(8,128)}, ...), condition=%wide.region_1.2_spmd.clone, body=%wide.region_0.1_spmd.clone.sunk | while | flops 28336136 | bytes 739997 | solution.py:28
  112.5 4.0 %all-to-all-start = ((f32[4,1,128]{2,1,0:T(1,128)}), f32[4,1,128]{2,1,0:T(1,128)S(1)}, u32[]{:S(2)}, u32[]{:S(2)}) async-start(f32[4,1,128]{2,1,0:T(1,128)} %broadcast_in_dim.32), calls=%async_computation | async-start | bytes 4096 | tf_op jit(solution)/shard_map/all_to_all | solution.py:33
  116.6 4.0 %all-to-all-done = f32[4,1,128]{2,1,0:T(1,128)S(1)} async-done(((f32[4,1,128]{2,1,0:T(1,128)}), f32[4,1,128]{2,1,0:T(1,128)S(1)}, u32[]{:S(2)}, u32[]{:S(2)}) %all-to-all-start) | async-done | bytes 2080 | tf_op jit(solution)/shard_map/all_to_all | solution.py:33
  121.1 18.0 %all-gather.2 = f32[256,384]{1,0:T(8,128)S(1)} all-gather(f32[16,384]{1,0:T(8,128)S(1)} %fusion.66), channel_id=4, replica_groups=mesh['area'=8,'hor'=16,'scen'=4] {'hor'}, dimensions={0}, use_global_device_ids=true | all-gather | bytes 417792 | tf_op jit(solution)/shard_map/all_gather | solution.py:15
  139.1 66.2 %while.33 = (s32[]{:T(128)}, f32[384,384]{1,0:T(8,128)S(1)}, f32[16,384]{1,0:T(8,128)S(1)}, s32[]{:T(128)}, f32[16,384,384]{2,1,0:T(8,128)}, /*index=5*/f32[16,16,384]{2,1,0:T(8,128)S(1)}, s32[]{:T(128)}, s32[]{:T(128)}) while((s32[]{:T(128)}, f32[384,384]{1,0:T(8,128)S(1)}, f32[16,384]{1,0:T(8,128)S(1)}, s32[]{:T(128)}, ...), condition=%wide.region_5.6_spmd.clone, body=%wide.region_4.5_spmd.clone.sunk | while | flops 707960832 | bytes 4279400 | solution.py:28
  139.1 1.7 fusion.128
  140.8 2.3 %convolution_select_fusion.2 = f32[384,384]{1,0:T(8,128)S(1)} fusion(f32[384,384]{1,0:T(8,128)S(1)} %copy.40, f32[16,384,384]{2,1,0:T(8,128)} %get-tuple-element.463, s32[]{:T(128)} %get-tuple-element.451, pred[]{:T(512)S(6)} %lt.101), kind=kOutput, calls=%fused_computation.10.clone.1 | convolution fusion | flops 679624704 | bytes 2359809 | tf_op jit(solution)/shard_map/while/body/eval_jaxpr/dot_general | solution.py:73
  145.0 2.3 %convolution_select_fusion.2 = f32[384,384]{1,0:T(8,128)S(1)} fusion(f32[384,384]{1,0:T(8,128)S(1)} %copy.40, f32[16,384,384]{2,1,0:T(8,128)} %get-tuple-element.463, s32[]{:T(128)} %get-tuple-element.451, pred[]{:T(512)S(6)} %lt.101), kind=kOutput, calls=%fused_computation.10.clone.1 | convolution fusion | flops 679624704 | bytes 2359809 | tf_op jit(solution)/shard_map/while/body/eval_jaxpr/dot_general | solution.py:73
  149.1 2.3 %convolution_select_fusion.2 = f32[384,384]{1,0:T(8,128)S(1)} fusion(f32[384,384]{1,0:T(8,128)S(1)} %copy.40, f32[16,384,384]{2,1,0:T(8,128)} %get-tuple-element.463, s32[]{:T(128)} %get-tuple-element.451, pred[]{:T(512)S(6)} %lt.101), kind=kOutput, calls=%fused_computation.10.clone.1 | convolution fusion | flops 679624704 | bytes 2359809 | tf_op jit(solution)/shard_map/while/body/eval_jaxpr/dot_general | solution.py:73
  153.3 2.3 %convolution_select_fusion.2 = f32[384,384]{1,0:T(8,128)S(1)} fusion(f32[384,384]{1,0:T(8,128)S(1)} %copy.40, f32[16,384,384]{2,1,0:T(8,128)} %get-tuple-element.463, s32[]{:T(128)} %get-tuple-element.451, pred[]{:T(512)S(6)} %lt.101), kind=kOutput, calls=%fused_computation.10.clone.1 | convolution fusion | flops 679624704 | bytes 2359809 | tf_op jit(solution)/shard_map/while/body/eval_jaxpr/dot_general | solution.py:73
  157.4 2.3 %convolution_select_fusion.2 = f32[384,384]{1,0:T(8,128)S(1)} fusion(f32[384,384]{1,0:T(8,128)S(1)} %copy.40, f32[16,384,384]{2,1,0:T(8,128)} %get-tuple-element.463, s32[]{:T(128)} %get-tuple-element.451, pred[]{:T(512)S(6)} %lt.101), kind=kOutput, calls=%fused_computation.10.clone.1 | convolution fusion | flops 679624704 | bytes 2359809 | tf_op jit(solution)/shard_map/while/body/eval_jaxpr/dot_general | solution.py:73
  161.5 2.3 %convolution_select_fusion.2 = f32[384,384]{1,0:T(8,128)S(1)} fusion(f32[384,384]{1,0:T(8,128)S(1)} %copy.40, f32[16,384,384]{2,1,0:T(8,128)} %get-tuple-element.463, s32[]{:T(128)} %get-tuple-element.451, pred[]{:T(512)S(6)} %lt.101), kind=kOutput, calls=%fused_computation.10.clone.1 | convolution fusion | flops 679624704 | bytes 2359809 | tf_op jit(solution)/shard_map/while/body/eval_jaxpr/dot_general | solution.py:73
  163.9 1.7 fusion.128
  165.7 2.3 %convolution_select_fusion.2 = f32[384,384]{1,0:T(8,128)S(1)} fusion(f32[384,384]{1,0:T(8,128)S(1)} %copy.40, f32[16,384,384]{2,1,0:T(8,128)} %get-tuple-element.463, s32[]{:T(128)} %get-tuple-element.451, pred[]{:T(512)S(6)} %lt.101), kind=kOutput, calls=%fused_computation.10.clone.1 | convolution fusion | flops 679624704 | bytes 2359809 | tf_op jit(solution)/shard_map/while/body/eval_jaxpr/dot_general | solution.py:73
  168.0 1.7 fusion.128
  169.8 2.3 %convolution_select_fusion.2 = f32[384,384]{1,0:T(8,128)S(1)} fusion(f32[384,384]{1,0:T(8,128)S(1)} %copy.40, f32[16,384,384]{2,1,0:T(8,128)} %get-tuple-element.463, s32[]{:T(128)} %get-tuple-element.451, pred[]{:T(512)S(6)} %lt.101), kind=kOutput, calls=%fused_computation.10.clone.1 | convolution fusion | flops 679624704 | bytes 2359809 | tf_op jit(solution)/shard_map/while/body/eval_jaxpr/dot_general | solution.py:73
  172.2 1.7 fusion.128
  174.0 2.3 %convolution_select_fusion.2 = f32[384,384]{1,0:T(8,128)S(1)} fusion(f32[384,384]{1,0:T(8,128)S(1)} %copy.40, f32[16,384,384]{2,1,0:T(8,128)} %get-tuple-element.463, s32[]{:T(128)} %get-tuple-element.451, pred[]{:T(512)S(6)} %lt.101), kind=kOutput, calls=%fused_computation.10.clone.1 | convolution fusion | flops 679624704 | bytes 2359809 | tf_op jit(solution)/shard_map/while/body/eval_jaxpr/dot_general | solution.py:73
  176.3 1.7 fusion.128
  178.1 2.3 %convolution_select_fusion.2 = f32[384,384]{1,0:T(8,128)S(1)} fusion(f32[384,384]{1,0:T(8,128)S(1)} %copy.40, f32[16,384,384]{2,1,0:T(8,128)} %get-tuple-element.463, s32[]{:T(128)} %get-tuple-element.451, pred[]{:T(512)S(6)} %lt.101), kind=kOutput, calls=%fused_computation.10.clone.1 | convolution fusion | flops 679624704 | bytes 2359809 | tf_op jit(solution)/shard_map/while/body/eval_jaxpr/dot_general | solution.py:73
  180.5 1.7 fusion.128
  182.2 2.3 %convolution_select_fusion.2 = f32[384,384]{1,0:T(8,128)S(1)} fusion(f32[384,384]{1,0:T(8,128)S(1)} %copy.40, f32[16,384,384]{2,1,0:T(8,128)} %get-tuple-element.463, s32[]{:T(128)} %get-tuple-element.451, pred[]{:T(512)S(6)} %lt.101), kind=kOutput, calls=%fused_computation.10.clone.1 | convolution fusion | flops 679624704 | bytes 2359809 | tf_op jit(solution)/shard_map/while/body/eval_jaxpr/dot_general | solution.py:73
  184.6 1.7 fusion.128
  186.4 2.3 %convolution_select_fusion.2 = f32[384,384]{1,0:T(8,128)S(1)} fusion(f32[384,384]{1,0:T(8,128)S(1)} %copy.40, f32[16,384,384]{2,1,0:T(8,128)} %get-tuple-element.463, s32[]{:T(128)} %get-tuple-element.451, pred[]{:T(512)S(6)} %lt.101), kind=kOutput, calls=%fused_computation.10.clone.1 | convolution fusion | flops 679624704 | bytes 2359809 | tf_op jit(solution)/shard_map/while/body/eval_jaxpr/dot_general | solution.py:73
  190.5 2.3 %convolution_select_fusion.2 = f32[384,384]{1,0:T(8,128)S(1)} fusion(f32[384,384]{1,0:T(8,128)S(1)} %copy.40, f32[16,384,384]{2,1,0:T(8,128)} %get-tuple-element.463, s32[]{:T(128)} %get-tuple-element.451, pred[]{:T(512)S(6)} %lt.101), kind=kOutput, calls=%fused_computation.10.clone.1 | convolution fusion | flops 679624704 | bytes 2359809 | tf_op jit(solution)/shard_map/while/body/eval_jaxpr/dot_general | solution.py:73
  194.6 2.3 %convolution_select_fusion.2 = f32[384,384]{1,0:T(8,128)S(1)} fusion(f32[384,384]{1,0:T(8,128)S(1)} %copy.40, f32[16,384,384]{2,1,0:T(8,128)} %get-tuple-element.463, s32[]{:T(128)} %get-tuple-element.451, pred[]{:T(512)S(6)} %lt.101), kind=kOutput, calls=%fused_computation.10.clone.1 | convolution fusion | flops 679624704 | bytes 2359809 | tf_op jit(solution)/shard_map/while/body/eval_jaxpr/dot_general | solution.py:73
  198.8 2.3 %convolution_select_fusion.2 = f32[384,384]{1,0:T(8,128)S(1)} fusion(f32[384,384]{1,0:T(8,128)S(1)} %copy.40, f32[16,384,384]{2,1,0:T(8,128)} %get-tuple-element.463, s32[]{:T(128)} %get-tuple-element.451, pred[]{:T(512)S(6)} %lt.101), kind=kOutput, calls=%fused_computation.10.clone.1 | convolution fusion | flops 679624704 | bytes 2359809 | tf_op jit(solution)/shard_map/while/body/eval_jaxpr/dot_general | solution.py:73
  202.9 2.3 %convolution_select_fusion.2 = f32[384,384]{1,0:T(8,128)S(1)} fusion(f32[384,384]{1,0:T(8,128)S(1)} %copy.40, f32[16,384,384]{2,1,0:T(8,128)} %get-tuple-element.463, s32[]{:T(128)} %get-tuple-element.451, pred[]{:T(512)S(6)} %lt.101), kind=kOutput, calls=%fused_computation.10.clone.1 | convolution fusion | flops 679624704 | bytes 2359809 | tf_op jit(solution)/shard_map/while/body/eval_jaxpr/dot_general | solution.py:73
  206.9 6.5 %all-to-all-start.1 = ((f32[8,1,2,16,128]{4,3,2,1,0:T(8,128)}), f32[8,1,2,16,128]{4,3,2,1,0:T(8,128)S(1)}, u32[]{:S(2)}, u32[]{:S(2)}) async-start(f32[8,1,2,16,128]{4,3,2,1,0:T(8,128)} %broadcast_in_dim.36), calls=%async_computation.1 | async-start | bytes 262144 | tf_op jit(solution)/shard_map/all_to_all | solution.py:33
  214.1 7.6 %all-to-all-done.1 = f32[8,1,2,16,128]{4,3,2,1,0:T(8,128)S(1)} async-done(((f32[8,1,2,16,128]{4,3,2,1,0:T(8,128)}), f32[8,1,2,16,128]{4,3,2,1,0:T(8,128)S(1)}, u32[]{:S(2)}, u32[]{:S(2)}) %all-to-all-start.1) | async-done | bytes 131104 | tf_op jit(solution)/shard_map/all_to_all | solution.py:33
  (132 shorter events, 51.4 us)
Async XLA Ops:
  7.2 104.5 %copy-start = (f32[1,384,128]{2,1,0:T(8,128)S(1)}, f32[1,384,128]{2,1,0:T(8,128)}, u32[]{:S(2)}) copy-start(f32[1,384,128]{2,1,0:T(8,128)} %param.22) | copy-start | bytes 589828
  7.2 14.0 %copy-start.7 = (s32[1,128]{1,0:T(1,128)S(1)}, s32[1,128]{1,0:T(1,128)}, u32[]{:S(2)}) copy-start(s32[1,128]{1,0:T(1,128)} %param.19) | copy-start | bytes 1540
  7.2 14.0 %copy-start.3 = (f32[1,2,16,384]{3,2,1,0:T(8,128)S(1)}, f32[1,2,16,384]{3,2,1,0:T(8,128)}, u32[]{:S(2)}) copy-start(f32[1,2,16,384]{3,2,1,0:T(8,128)} %param.24) | copy-start | bytes 147460
  7.2 14.0 %copy-start.4 = (f32[1,2,16,128]{3,2,1,0:T(8,128)S(1)}, f32[1,2,16,128]{3,2,1,0:T(8,128)}, u32[]{:S(2)}) copy-start(f32[1,2,16,128]{3,2,1,0:T(8,128)} %param.26) | copy-start | bytes 49156
  7.2 14.0 %copy-start.1 = (f32[1,2,16,128]{3,2,1,0:T(8,128)S(1)}, f32[1,2,16,128]{3,2,1,0:T(8,128)}, u32[]{:S(2)}) copy-start(f32[1,2,16,128]{3,2,1,0:T(8,128)} %param.27) | copy-start | bytes 49156
  7.2 104.4 %copy-start.6 = (f32[1,128]{1,0:T(1,128)S(1)}, f32[1,128]{1,0:T(1,128)}, u32[]{:S(2)}) copy-start(f32[1,128]{1,0:T(1,128)} %param.23) | copy-start | bytes 1540
  7.2 109.3 %copy-start.5 = (f32[1,384]{1,0:T(1,128)S(1)}, f32[1,384]{1,0:T(1,128)}, u32[]{:S(2)}) copy-start(f32[1,384]{1,0:T(1,128)} %param.21) | copy-start | bytes 4612
  7.2 113.4 %copy-start.2 = (f32[1,2,16,384]{3,2,1,0:T(8,128)S(1)}, f32[1,2,16,384]{3,2,1,0:T(8,128)}, u32[]{:S(2)}) copy-start(f32[1,2,16,384]{3,2,1,0:T(8,128)} %param.25) | copy-start | bytes 147460
  7.3 79.5 %all-gather.5.cloned.1.call-start = ((), (), s32[]{:S(2)}) async-start(), calls=%async_computation.2 | async-start | bytes 10027008 | tf_op jit(solution)/shard_map/all_gather | solution.py:15
  112.5 8.0 %all-to-all-start = ((f32[4,1,128]{2,1,0:T(1,128)}), f32[4,1,128]{2,1,0:T(1,128)S(1)}, u32[]{:S(2)}, u32[]{:S(2)}) async-start(f32[4,1,128]{2,1,0:T(1,128)} %broadcast_in_dim.32), calls=%async_computation | async-start | bytes 4096 | tf_op jit(solution)/shard_map/all_to_all | solution.py:33
  139.1 74.3 %copy-start.8 = (s32[1,3]{1,0:T(1,128)S(1)}, s32[1,3]{1,0:T(1,128)}, u32[]{:S(2)}) copy-start(s32[1,3]{1,0:T(1,128)} %param.20) | copy-start | bytes 40
  206.9 14.8 %all-to-all-start.1 = ((f32[8,1,2,16,128]{4,3,2,1,0:T(8,128)}), f32[8,1,2,16,128]{4,3,2,1,0:T(8,128)S(1)}, u32[]{:S(2)}, u32[]{:S(2)}) async-start(f32[8,1,2,16,128]{4,3,2,1,0:T(8,128)} %broadcast_in_dim.36), calls=%async_computation.1 | async-start | bytes 262144 | tf_op jit(solution)/shard_map/all_to_all | solution.py:33
Sparse Core Ops, SparseCore 0:
  15.8 70.8 all-gather.4
where the time goes:
time: 232 us; the launch traced here: 229 us
  matrix products  90.2 us (39%)
  waiting for transfers between devices  50 us (22%)
  blocking collectives  44.7 us (19%)
  between operations  22.2 us (10%)
  starting transfers between devices  10.5 us (5%)
  local copies, waits for them, and re-layouts  5.54 us (2%)
  other arithmetic  4.74 us (2%)
    dot_general x32, matrix products, product(): jnp.dot(left, right, precision=highest, preferred_element_type=jnp.float32)  61.3 us
    all_gather x2, blocking collectives, carried_in(): everything = jax.tree.map(lambda part: lax.all_gather(part, axis), shard)  44.7 us
    all_gather x1, waiting for transfers between devices, carried_in(): everything = jax.tree.map(lambda part: lax.all_gather(part, axis), shard)  38.4 us
    dot_general x17, matrix products, product_transposed(): lax.dot_general(left, right, (((1,), (1,)), ((), ())), precision=highest,...  27.7 us
    all_to_all x2, waiting for transfers between devices, sent_to_all(): return lax.all_to_all(copies, axis, split_axis=0, concat_axis=0, tiled=True)  11.6 us
    all_to_all x2, starting transfers between devices, sent_to_all(): return lax.all_to_all(copies, axis, split_axis=0, concat_axis=0, tiled=True)  10.4 us
  transfers between devices with their start and end apart: 3, of which 3 were waited for; matrix products, arithmetic and copies ran while one was open for 1% of the time, Pallas kernels for 0%

commit v1 on v0

v1 whole, which is shorter than its diff:
```python
import functools

import jax
import jax.numpy as jnp
from jax import lax
from jax.experimental import pallas as pl
from jax.experimental.pallas import tpu as pltpu
from jax.sharding import PartitionSpec as P

STEP = 16
NNB = 3

highest = lax.Precision.HIGHEST


def product(left, right):
    return jnp.dot(left, right, precision=highest, preferred_element_type=jnp.float32)


def product_transposed(left, right):
    return lax.dot_general(
        left, right, (((1,), (1,)), ((), ())), precision=highest, preferred_element_type=jnp.float32
    )


def kernel(
    segments,
    sharers,
    areas,
    offsets_ref,
    adjacency_ref,
    diagonal_ref,
    band_ref,
    index_ref,
    start_ref,
    matrix_ref,
    penalty_ref,
    cost_ref,
    noise_ref,
    consensus_ref,
    dual_ref,
    trajectory_ref,
    agreed_ref,
    updated_ref,
    grad_buf,
    pack_buf,
    pack_in,
    noise_buf,
    noise_in,
    part_buf,
    part_in,
    mean_buf,
    mean_in,
    costate_buf,
    force_buf,
    state_buf,
    state_in,
    boundary_buf,
    boundary_in,
    pack_send,
    pack_recv,
    noise_send,
    noise_recv,
    part_send,
    part_recv,
    mean_send,
    mean_recv,
    state_send,
    state_recv,
    boundary_send,
    boundary_recv,
):
    place = lax.axis_index("hor")
    share = lax.axis_index("scen")
    area = lax.axis_index("area")
    scens = segments
    extent = diagonal_ref.shape[-1]

    barrier = pltpu.get_barrier_semaphore()

    def greet(axis, own, count):
        def body(k, carry):
            pl.semaphore_signal(
                barrier,
                inc=1,
                device_id={axis: lax.rem(own + k, count)},
                device_id_type=pl.DeviceIdType.MESH,
            )
            return carry

        lax.fori_loop(1, count, body, 0)

    greet("hor", place, segments)
    greet("scen", share, sharers)
    greet("area", area, areas)

    selection = (
        lax.broadcasted_iota(jnp.int32, (extent, index_ref.shape[-1]), 0) == index_ref[...]
    ).astype(jnp.float32)
    for t in range(2):
        grad_buf[pl.ds(t * scens, scens), :] = cost_ref[0, t] + product_transposed(
            dual_ref[0, t] - consensus_ref[0, t], selection
        )
        part_buf[pl.ds(t, 1), :] = jnp.sum(
            grad_buf[pl.ds(t * scens, scens), :], axis=0, keepdims=True
        )
    lane = lax.broadcasted_iota(jnp.int32, (1, extent), 1)
    rows = []
    for t in range(2):
        up = jnp.zeros((1, extent), jnp.float32)
        down = jnp.zeros((1, extent), jnp.float32)
        for b in range(band_ref.shape[2]):
            coef = band_ref[0, t, pl.ds(b, 1), :]
            ahead = jnp.where(offsets_ref[0, b] > 0, 1.0, 0.0)
            up = up + ahead * coef
            down = down + (1.0 - ahead) * coef
        up = jnp.where(lane >= extent - STEP, 0.0, up)
        down = jnp.where(lane < STEP, 0.0, down)
        rows.append((diagonal_ref[0, pl.ds(t, 1), :], up, down))
    for s in range(scens):
        for t in range(2):
            pack_buf[s, pl.ds(t, 1), :] = grad_buf[pl.ds(t * scens + s, 1), :]
            noise_buf[s, pl.ds(t, 1), :] = noise_ref[0, t, pl.ds(s, 1), :]
            for c in range(3):
                pack_buf[s, pl.ds(2 + 3 * t + c, 1), :] = rows[t][c]
    pack_in[place] = pack_buf[place]
    noise_in[place] = noise_buf[place]
    part_in[share] = part_buf[...]

    pl.semaphore_wait(barrier, segments + sharers + areas - 3)

    def copy_to(axis, own, other, source, target, send, recv):
        return pltpu.make_async_remote_copy(
            src_ref=source,
            dst_ref=target.at[own],
            send_sem=send.at[other],
            recv_sem=recv.at[own],
            device_id={axis: other},
            device_id_type=pl.DeviceIdType.MESH,
        )

    def each(count, own, action):
        def body(k, carry):
            action(lax.rem(own + k, count))
            return carry

        lax.fori_loop(1, count, body, 0)

    def part_copy(other):
        return copy_to("scen", share, other, part_buf, part_in, part_send, part_recv)

    def pack_copy(other):
        return copy_to("hor", place, other, pack_buf.at[other], pack_in, pack_send, pack_recv)

    def noise_copy(other):
        return copy_to("hor", place, other, noise_buf.at[other], noise_in, noise_send, noise_recv)

    def mean_copy(other):
        return copy_to("hor", place, other, mean_buf, mean_in, mean_send, mean_recv)

    def state_copy(other):
        return copy_to("hor", place, other, state_buf.at[other], state_in, state_send, state_recv)

    def boundary_copy(other):
        return copy_to(
            "area", area, other, boundary_buf, boundary_in, boundary_send, boundary_recv
        )

    def arrived(axis, other, source, target, send, recv):
        pltpu.make_async_remote_copy(
            src_ref=source,
            dst_ref=target.at[other],
            send_sem=send.at[other],
            recv_sem=recv.at[other],
            device_id={axis: other},
            device_id_type=pl.DeviceIdType.MESH,
        ).wait_recv()

    each(sharers, share, lambda o: part_copy(o).start())
    each(segments, place, lambda o: pack_copy(o).start())
    each(
        sharers, share, lambda o: arrived("scen", o, part_buf, part_in, part_send, part_recv)
    )
    total = part_in[0]
    for k in range(1, sharers):
        total = total + part_in[k]
    mean_buf[...] = total * (1.0 / (scens * sharers))
    mean_in[place] = mean_buf[...]
    each(segments, place, lambda o: mean_copy(o).start())
    each(segments, place, lambda o: noise_copy(o).start())
    each(
        segments,
        place,
        lambda o: arrived("hor", o, pack_buf.at[o], pack_in, pack_send, pack_recv),
    )
    each(segments, place, lambda o: arrived("hor", o, mean_buf, mean_in, mean_send, mean_recv))

    first = lax.broadcasted_iota(jnp.int32, (8, extent), 0) == 0

    def wide(row):
        return jnp.broadcast_to(row, (8, extent))

    def back(k, costate):
        h = segments - 1 - k
        for j in (1, 0):
            costate_buf[pl.ds(2 * h + j, 1), :] = costate[0:1, :]
            diag, up, down = (
                wide(pack_in[h, pl.ds(2 + 3 * j + c, 1), :]) for c in range(3)
            )
            grad = jnp.where(
                first, wide(pack_in[h, pl.ds(j, 1), :]), wide(mean_in[h, pl.ds(j, 1), :])
            )
            if j == 0:
                costate_buf[pl.ds(2 * segments, 8), :] = costate
            costate = (
                (diag * costate + grad)
                + pltpu.roll(up * costate, STEP, 1)
                + pltpu.roll(down * costate, extent - STEP, 1)
            )
        return costate

    lax.fori_loop(0, segments, back, jnp.zeros((8, extent), jnp.float32))

    controls = -product(costate_buf[...], matrix_ref[0]) / penalty_ref[...]
    shared = controls[2 * segments + 1 : 2 * segments + 2, :]
    controls = controls[0 : 2 * segments, :]
    at_start = lax.broadcasted_iota(jnp.int32, controls.shape, 0) == 0
    controls = jnp.where(at_start, jnp.broadcast_to(shared, controls.shape), controls)
    force_buf[...] = product_transposed(controls, matrix_ref[0])
    each(
        segments,
        place,
        lambda o: arrived("hor", o, noise_buf.at[o], noise_in, noise_send, noise_recv),
    )

    def ahead_step(h, state):
        for j in (0, 1):
            state_buf[h, pl.ds(j, 1), :] = state[0:1, :]
            diag, up, down = (
                wide(pack_in[h, pl.ds(2 + 3 * j + c, 1), :]) for c in range(3)
            )
            force = wide(force_buf[pl.ds(2 * h + j, 1), :] + noise_in[h, pl.ds(j, 1), :])
            state = (
                (diag * state + force)
                + up * pltpu.roll(state, extent - STEP, 1)
                + down * pltpu.roll(state, STEP, 1)
            )

        @pl.when(h != place)
        def _():
            state_copy(h).start()

        return state

    lax.fori_loop(0, segments, ahead_step, wide(start_ref[...]))
    state_in[place] = state_buf[place]
    each(
        segments,
        place,
        lambda o: arrived("hor", o, state_buf.at[o], state_in, state_send, state_recv),
    )
    for s in range(scens):
        for t in range(2):
            trajectory_ref[0, t, pl.ds(s, 1), :] = state_in[s, pl.ds(t, 1), :]
    for t in range(2):
        boundary_buf[t] = product(trajectory_ref[0, t], selection)
    each(areas, area, lambda o: boundary_copy(o).start())
    boundary_in[area] = boundary_buf[...]
    each(
        areas,
        area,
        lambda o: arrived("area", o, boundary_buf, boundary_in, boundary_send, boundary_recv),
    )
    summed = boundary_buf[...]
    for n in range(areas):
        weight = jnp.float32(0.0)
        for j in range(NNB):
            weight = weight + jnp.where(adjacency_ref[0, j] == n, 1.0, 0.0)
        summed = summed + weight * boundary_in[n]
    agreed = summed * (1.0 / (NNB + 1))
    agreed_ref[0] = agreed
    updated_ref[0] = dual_ref[0] + boundary_buf[...] - agreed

    each(sharers, share, lambda o: part_copy(o).wait_send())

    def drain(o):
        pack_copy(o).wait_send()
        mean_copy(o).wait_send()
        noise_copy(o).wait_send()
        state_copy(o).wait_send()

    each(segments, place, drain)
    each(areas, area, lambda o: boundary_copy(o).wait_send())


def per_device(
    diagonal,
    band_coef,
    band_offsets,
    boundary_index,
    adjacency,
    start_state,
    input_matrix,
    input_penalty,
    linear_cost,
    disturbance,
    consensus,
    dual_values,
):
    segments = lax.axis_size("hor")
    sharers = lax.axis_size("scen")
    areas = lax.axis_size("area")
    extent = diagonal.shape[-1]
    vmem = pl.BlockSpec(memory_space=pltpu.VMEM)
    smem = pl.BlockSpec(memory_space=pltpu.SMEM)
    real = jnp.float32
    scratch = [
        pltpu.VMEM((2 * segments, extent), real),
        pltpu.VMEM((segments, 8, extent), real),
        pltpu.VMEM((segments, 8, extent), real),
        pltpu.VMEM((segments, 2, extent), real),
        pltpu.VMEM((segments, 2, extent), real),
        pltpu.VMEM((2, extent), real),
        pltpu.VMEM((sharers, 2, extent), real),
        pltpu.VMEM((2, extent), real),
        pltpu.VMEM((segments, 2, extent), real),
        pltpu.VMEM((2 * segments + 8, extent), real),
        pltpu.VMEM((2 * segments, extent), real),
        pltpu.VMEM((segments, 2, extent), real),
        pltpu.VMEM((segments, 2, extent), real),
        pltpu.VMEM(dual_values.shape[1:], real),
        pltpu.VMEM((areas, *dual_values.shape[1:]), real),
    ]
    for count in (segments, segments, sharers, segments, segments, areas):
        scratch += [pltpu.SemaphoreType.DMA((count,)), pltpu.SemaphoreType.DMA((count,))]
    return pl.pallas_call(
        functools.partial(kernel, segments, sharers, areas),
        out_shape=(
            jax.ShapeDtypeStruct(linear_cost.shape, real),
            jax.ShapeDtypeStruct(dual_values.shape, real),
            jax.ShapeDtypeStruct(dual_values.shape, real),
        ),
        in_specs=[smem] * 2 + [vmem] * 10,
        out_specs=(vmem,) * 3,
        scratch_shapes=scratch,
        compiler_params=pltpu.CompilerParams(collective_id=0, has_side_effects=True),
    )(
        band_offsets,
        adjacency,
        diagonal,
        band_coef,
        boundary_index,
        start_state,
        input_matrix,
        input_penalty,
        linear_cost,
        disturbance,
        consensus,
        dual_values,
    )


def solution(mesh):
    in_specs = (
        P("area", "hor", None),
        P("area", "hor", None, None),
        P("area", None),
        P("area", None),
        P("area", None),
        P("area", None),
        P("area", None, None),
        P("area", None),
        P("area", "hor", "scen", None),
        P("area", "hor", "scen", None),
        P("area", "hor", "scen", None),
        P("area", "hor", "scen", None),
    )
    out_specs = (
        P("area", "hor", "scen", None),
        P("area", "hor", "scen", None),
        P("area", "hor", "scen", None),
    )
    return jax.shard_map(
        per_device, mesh=mesh, in_specs=in_specs, out_specs=out_specs, check_vma=False
    )
```

time: 232 us -> 44.6 us (0.19)
  matrix products: 90.2 us -> 0 us
  waiting for transfers between devices: 50 us -> 0 us
  blocking collectives: 44.7 us -> 0 us
  Pallas kernels: 0 us -> 40.8 us
  between operations: 22.2 us -> 0.65 us
  starting transfers between devices: 10.5 us -> 0 us
  other arithmetic: 4.74 us -> 0 us
  local copies, waits for them, and re-layouts: 5.54 us -> 2.76 us
    dot_general x54 -> x0, matrix products: 90.2 us -> none  [the longest x32 61.3 us: product(): jnp.dot(left, right, precision=highest, preferred_element_type=jnp.float32)]
    all_gather x2 -> x0, blocking collectives: 44.7 us -> none  [carried_in(): everything = jax.tree.map(lambda part: lax.all_gather(part, axis), shard)]
    pallas_call x0 -> x1, Pallas kernels: none -> 40.8 us  [per_device(): pl.pallas_call(functools.partial(kernel, segments, sharers, areas), out_s...]
    all_gather x1 -> x0, waiting for transfers between devices: 38.4 us -> none  [carried_in(): everything = jax.tree.map(lambda part: lax.all_gather(part, axis), shard)]
    all_to_all x2 -> x0, waiting for transfers between devices: 11.6 us -> none  [sent_to_all(): return lax.all_to_all(copies, axis, split_axis=0, concat_axis=0, tiled=True)]
    all_to_all x2 -> x0, starting transfers between devices: 10.4 us -> none  [sent_to_all(): return lax.all_to_all(copies, axis, split_axis=0, concat_axis=0, tiled=True)]
    slice x3 -> x0, local copies, waits for them, and re-layouts: 3.16 us -> none  [the longest x1 1.45 us: backward_apply(): offsets[band_index]]
    unnamed x18 -> x7, local copies, waits for them, and re-layouts: 0.04 us -> 2.76 us
  transfers between devices with their start and end apart: 3 -> 0, of which waited for: 3 -> 0; matrix products, arithmetic and copies ran while one was open for 1% -> 0% of each run, Pallas kernels for 0% -> 0%
where the time goes in v1:
time: 44.6 us; the launch traced here: 44.3 us
  Pallas kernels  40.8 us (91%)
  local copies, waits for them, and re-layouts  2.76 us (6%)
  between operations  0.65 us (1%)
    pallas_call x1, Pallas kernels, per_device(): pl.pallas_call(functools.partial(kernel, segments, sharers, areas), out_s...  40.8 us
    unnamed x7, local copies, waits for them, and re-layouts  2.76 us

profile of v1, /device:TPU:1, one launch (start us, length us, event | category | flops | bytes accessed | tf_op | source)
XLA Modules:
  0.0 44.3 jit_solution(5379745543185740988)
XLA Ops:
  0.6 40.8 %shard_map.139 = (f32[1,2,16,384]{3,2,1,0:T(8,128)}, f32[1,2,16,128]{3,2,1,0:T(8,128)}, f32[1,2,16,128]{3,2,1,0:T(8,128)}) custom-call(s32[1,4]{1,0:T(1,128)} %offsets_ref.1, s32[1,3]{1,0:T(1,128)} %adjacency_ref.1, f32[1,2,384]{2,1,0:T(2,128)} %diagonal_ref.1, f32[1,2,4,384]{3,2,1,0:T(4,128)} %band_ref.1, s32[1,128]{1,0:T(1,128)} %index_ref.1, ...), custom_call_target="tpu_custom_call" | custom-call | tf_op jit(solution)/shard_map/pallas_call | solution.py:336
  41.5 0.0 copy-start.1
  41.5 1.4 %copy.18 = f32[1,2,16,384]{3,2,1,0:T(8,128)} copy(f32[1,2,16,384]{3,2,1,0:T(8,128)} %get-tuple-element.6) | data formatting | bytes 98304
  42.9 0.0 copy-done.1
  42.9 0.0 copy-start
  42.9 0.6 %copy.19 = f32[1,2,16,128]{3,2,1,0:T(8,128)} copy(f32[1,2,16,128]{3,2,1,0:T(8,128)S(1)} %copy-done.1) | data formatting | bytes 32768
  43.5 0.1 copy-done
  43.7 0.6 %copy.20 = f32[1,2,16,128]{3,2,1,0:T(8,128)} copy(f32[1,2,16,128]{3,2,1,0:T(8,128)S(1)} %copy-done) | data formatting | bytes 32768
Async XLA Ops:
  41.5 1.4 %copy-start.1 = (f32[1,2,16,128]{3,2,1,0:T(8,128)S(1)}, f32[1,2,16,128]{3,2,1,0:T(8,128)}, u32[]{:S(2)}) copy-start(f32[1,2,16,128]{3,2,1,0:T(8,128)} %get-tuple-element.7) | copy-start | bytes 49156
  42.9 0.7 %copy-start = (f32[1,2,16,128]{3,2,1,0:T(8,128)S(1)}, f32[1,2,16,128]{3,2,1,0:T(8,128)}, u32[]{:S(2)}) copy-start(f32[1,2,16,128]{3,2,1,0:T(8,128)} %get-tuple-element.8) | copy-start | bytes 49156

commit v2 on v1

--- a/solution.py
+++ b/solution.py
@@ -27,6 +27,21 @@
     segments,
     sharers,
     areas,
+    offsets_hbm,
+    adjacency_hbm,
+    diagonal_hbm,
+    band_hbm,
+    index_hbm,
+    start_hbm,
+    matrix_hbm,
+    penalty_hbm,
+    cost_hbm,
+    noise_hbm,
+    consensus_hbm,
+    dual_hbm,
+    trajectory_hbm,
+    agreed_hbm,
+    updated_hbm,
     offsets_ref,
     adjacency_ref,
     diagonal_ref,
@@ -43,6 +58,7 @@
     agreed_ref,
     updated_ref,
     grad_buf,
+    coef_in,
     pack_buf,
     pack_in,
     noise_buf,
@@ -57,6 +73,10 @@
     state_in,
     boundary_buf,
     boundary_in,
+    fetch_sem,
+    coef_send,
+    pass_send,
+    coef_recv,
     pack_send,
     pack_recv,
     noise_send,
@@ -94,6 +114,30 @@
     greet("scen", share, sharers)
     greet("area", area, areas)
 
+    fetches = [
+        pltpu.make_async_copy(source, target, fetch_sem.at[k])
+        for k, (source, target) in enumerate(
+            (
+                (offsets_hbm, offsets_ref),
+                (band_hbm, band_ref),
+                (diagonal_hbm, diagonal_ref),
+                (index_hbm, index_ref),
+                (dual_hbm, dual_ref),
+                (consensus_hbm, consensus_ref),
+                (cost_hbm, cost_ref),
+                (noise_hbm, noise_ref),
+                (matrix_hbm, matrix_ref),
+                (penalty_hbm, penalty_ref),
+                (start_hbm, start_ref),
+                (adjacency_hbm, adjacency_ref),
+            )
+        )
+    ]
+    for fetch in fetches:
+        fetch.start()
+    for fetch in fetches[:8]:
+        fetch.wait()
+
     selection = (
         lax.broadcasted_iota(jnp.int32, (extent, index_ref.shape[-1]), 0) == index_ref[...]
     ).astype(jnp.float32)
@@ -105,7 +149,6 @@
             grad_buf[pl.ds(t * scens, scens), :], axis=0, keepdims=True
         )
     lane = lax.broadcasted_iota(jnp.int32, (1, extent), 1)
-    rows = []
     for t in range(2):
         up = jnp.zeros((1, extent), jnp.float32)
         down = jnp.zeros((1, extent), jnp.float32)
@@ -116,13 +159,12 @@
             down = down + (1.0 - ahead) * coef
         up = jnp.where(lane >= extent - STEP, 0.0, up)
         down = jnp.where(lane < STEP, 0.0, down)
-        rows.append((diagonal_ref[0, pl.ds(t, 1), :], up, down))
+        for c, row in enumerate((diagonal_ref[0, pl.ds(t, 1), :], up, down)):
+            coef_in[place, c, pl.ds(t, 1), :] = row
     for s in range(scens):
         for t in range(2):
             pack_buf[s, pl.ds(t, 1), :] = grad_buf[pl.ds(t * scens + s, 1), :]
             noise_buf[s, pl.ds(t, 1), :] = noise_ref[0, t, pl.ds(s, 1), :]
-            for c in range(3):
-                pack_buf[s, pl.ds(2 + 3 * t + c, 1), :] = rows[t][c]
     pack_in[place] = pack_buf[place]
     noise_in[place] = noise_buf[place]
     part_in[share] = part_buf[...]
@@ -145,6 +187,25 @@
             return carry
 
         lax.fori_loop(1, count, body, 0)
+
+    partner = place + 1 - 2 * lax.rem(place, 2)
+
+    def coef_copy(slot, other, sem):
+        return pltpu.make_async_remote_copy(
+            src_ref=coef_in.at[slot],
+            dst_ref=coef_in.at[slot],
+            send_sem=sem,
+            recv_sem=coef_recv.at[slot],
+            device_id={"hor": other},
+            device_id_type=pl.DeviceIdType.MESH,
+        )
+
+    def each_chip(action):
+        def body(k, carry):
+            action(lax.rem(place + 2 * k, segments))
+            return carry
+
+        lax.fori_loop(1, segments // 2, body, 0)
 
     def part_copy(other):
         return copy_to("scen", share, other, part_buf, part_in, part_send, part_recv)
@@ -177,6 +238,8 @@
         ).wait_recv()
 
     each(sharers, share, lambda o: part_copy(o).start())
+    each_chip(lambda o: coef_copy(place, o, coef_send.at[o]).start())
+    coef_copy(place, partner, pass_send.at[place]).start()
     each(segments, place, lambda o: pack_copy(o).start())
     each(
         sharers, share, lambda o: arrived("scen", o, part_buf, part_in, part_send, part_recv)
@@ -188,12 +251,18 @@
     mean_in[place] = mean_buf[...]
     each(segments, place, lambda o: mean_copy(o).start())
     each(segments, place, lambda o: noise_copy(o).start())
-    each(
-        segments,
-        place,
-        lambda o: arrived("hor", o, pack_buf.at[o], pack_in, pack_send, pack_recv),
-    )
-    each(segments, place, lambda o: arrived("hor", o, mean_buf, mean_in, mean_send, mean_recv))
+
+    def relay(o):
+        coef_copy(o, o, coef_send.at[o]).wait_recv()
+        coef_copy(o, partner, pass_send.at[o]).start()
+
+    each_chip(relay)
+    coef_copy(partner, partner, pass_send.at[partner]).wait_recv()
+    each_chip(
+        lambda o: coef_copy(
+            o + partner - place, partner, pass_send.at[o + partner - place]
+        ).wait_recv()
+    )
 
     first = lax.broadcasted_iota(jnp.int32, (8, extent), 0) == 0
 
@@ -202,10 +271,16 @@
 
     def back(k, costate):
         h = segments - 1 - k
+
+        @pl.when(h != place)
+        def _():
+            arrived("hor", h, pack_buf.at[h], pack_in, pack_send, pack_recv)
+            arrived("hor", h, mean_buf, mean_in, mean_send, mean_recv)
+
         for j in (1, 0):
             costate_buf[pl.ds(2 * h + j, 1), :] = costate[0:1, :]
             diag, up, down = (
-                wide(pack_in[h, pl.ds(2 + 3 * j + c, 1), :]) for c in range(3)
+                wide(coef_in[h, c, pl.ds(j, 1), :]) for c in range(3)
             )
             grad = jnp.where(
                 first, wide(pack_in[h, pl.ds(j, 1), :]), wide(mean_in[h, pl.ds(j, 1), :])
@@ -221,6 +296,8 @@
 
     lax.fori_loop(0, segments, back, jnp.zeros((8, extent), jnp.float32))
 
+    for fetch in fetches[8:]:
+        fetch.wait()
     controls = -product(costate_buf[...], matrix_ref[0]) / penalty_ref[...]
     shared = controls[2 * segments + 1 : 2 * segments + 2, :]
     controls = controls[0 : 2 * segments, :]
@@ -237,7 +314,7 @@
         for j in (0, 1):
             state_buf[h, pl.ds(j, 1), :] = state[0:1, :]
             diag, up, down = (
-                wide(pack_in[h, pl.ds(2 + 3 * j + c, 1), :]) for c in range(3)
+                wide(coef_in[h, c, pl.ds(j, 1), :]) for c in range(3)
             )
             force = wide(force_buf[pl.ds(2 * h + j, 1), :] + noise_in[h, pl.ds(j, 1), :])
             state = (
@@ -262,6 +339,8 @@
     for s in range(scens):
         for t in range(2):
             trajectory_ref[0, t, pl.ds(s, 1), :] = state_in[s, pl.ds(t, 1), :]
+    put_state = pltpu.make_async_copy(trajectory_ref, trajectory_hbm, fetch_sem.at[0])
+    put_state.start()
     for t in range(2):
         boundary_buf[t] = product(trajectory_ref[0, t], selection)
     each(areas, area, lambda o: boundary_copy(o).start())
@@ -280,8 +359,19 @@
     agreed = summed * (1.0 / (NNB + 1))
     agreed_ref[0] = agreed
     updated_ref[0] = dual_ref[0] + boundary_buf[...] - agreed
+    put_agreed = pltpu.make_async_copy(agreed_ref, agreed_hbm, fetch_sem.at[1])
+    put_updated = pltpu.make_async_copy(updated_ref, updated_hbm, fetch_sem.at[2])
+    put_agreed.start()
+    put_updated.start()
 
     each(sharers, share, lambda o: part_copy(o).wait_send())
+
+    def drain_chip(o):
+        coef_copy(place, o, coef_send.at[o]).wait_send()
+        coef_copy(o, partner, pass_send.at[o]).wait_send()
+
+    each_chip(drain_chip)
+    coef_copy(place, partner, pass_send.at[place]).wait_send()
 
     def drain(o):
         pack_copy(o).wait_send()
@@ -291,6 +381,9 @@
 
     each(segments, place, drain)
     each(areas, area, lambda o: boundary_copy(o).wait_send())
+    put_state.wait()
+    put_agreed.wait()
+    put_updated.wait()
 
 
 def per_device(
@@ -311,13 +404,35 @@
     sharers = lax.axis_size("scen")
     areas = lax.axis_size("area")
     extent = diagonal.shape[-1]
-    vmem = pl.BlockSpec(memory_space=pltpu.VMEM)
-    smem = pl.BlockSpec(memory_space=pltpu.SMEM)
+    anywhere = pl.BlockSpec(memory_space=pl.ANY)
     real = jnp.float32
     scratch = [
+        pltpu.SMEM(band_offsets.shape, jnp.int32),
+        pltpu.SMEM(adjacency.shape, jnp.int32),
+    ]
+    scratch += [
+        pltpu.VMEM(held.shape, held.dtype)
+        for held in (
+            diagonal,
+            band_coef,
+            boundary_index,
+            start_state,
+            input_matrix,
+            input_penalty,
+            linear_cost,
+            disturbance,
+            consensus,
+            dual_values,
+            linear_cost,
+            dual_values,
+            dual_values,
+        )
+    ]
+    scratch += [
         pltpu.VMEM((2 * segments, extent), real),
-        pltpu.VMEM((segments, 8, extent), real),
-        pltpu.VMEM((segments, 8, extent), real),
+        pltpu.VMEM((segments, 3, 2, extent), real),
+        pltpu.VMEM((segments, 2, extent), real),
+        pltpu.VMEM((segments, 2, extent), real),
         pltpu.VMEM((segments, 2, extent), real),
         pltpu.VMEM((segments, 2, extent), real),
         pltpu.VMEM((2, extent), real),
@@ -331,6 +446,8 @@
         pltpu.VMEM(dual_values.shape[1:], real),
         pltpu.VMEM((areas, *dual_values.shape[1:]), real),
     ]
+    scratch += [pltpu.SemaphoreType.DMA((12,))]
+    scratch += [pltpu.SemaphoreType.DMA((segments,)) for _ in range(3)]
     for count in (segments, segments, sharers, segments, segments, areas):
         scratch += [pltpu.SemaphoreType.DMA((count,)), pltpu.SemaphoreType.DMA((count,))]
     return pl.pallas_call(
@@ -340,8 +457,8 @@
             jax.ShapeDtypeStruct(dual_values.shape, real),
             jax.ShapeDtypeStruct(dual_values.shape, real),
         ),
-        in_specs=[smem] * 2 + [vmem] * 10,
-        out_specs=(vmem,) * 3,
+        in_specs=[anywhere] * 12,
+        out_specs=(anywhere,) * 3,
         scratch_shapes=scratch,
         compiler_params=pltpu.CompilerParams(collective_id=0, has_side_effects=True),
     )(

time: 44.6 us -> 41.9 us (0.939)
  Pallas kernels: 40.8 us -> 38.2 us
    pallas_call x1, Pallas kernels: 40.8 us -> 38.2 us  [per_device(): pl.pallas_call(functools.partial(kernel, segments, sharers, areas), out_s...]
where the time goes in v2:
time: 41.9 us; the launch traced here: 41.6 us
  Pallas kernels  38.2 us (91%)
  local copies, waits for them, and re-layouts  2.76 us (7%)
  between operations  0.65 us (2%)
    pallas_call x1, Pallas kernels, per_device(): pl.pallas_call(functools.partial(kernel, segments, sharers, areas), out_s...  38.2 us
    unnamed x7, local copies, waits for them, and re-layouts  2.76 us

profile of v2, /device:TPU:1, one launch (start us, length us, event | category | flops | bytes accessed | tf_op | source)
XLA Modules:
  0.0 41.6 jit_solution(5361819070462878081)
XLA Ops:
  0.6 38.2 %shard_map.139 = (f32[1,2,16,384]{3,2,1,0:T(8,128)}, f32[1,2,16,128]{3,2,1,0:T(8,128)}, f32[1,2,16,128]{3,2,1,0:T(8,128)}) custom-call(s32[1,4]{1,0:T(1,128)} %offsets_hbm.1, s32[1,3]{1,0:T(1,128)} %adjacency_hbm.1, f32[1,2,384]{2,1,0:T(2,128)} %diagonal_hbm.1, f32[1,2,4,384]{3,2,1,0:T(4,128)} %band_hbm.1, s32[1,128]{1,0:T(1,128)} %index_hbm.1, ...), custom_call_target="tpu_custom_call" | custom-call | tf_op jit(solution)/shard_map/pallas_call | solution.py:453
  38.9 0.0 copy-start.1
  38.9 1.4 %copy.18 = f32[1,2,16,384]{3,2,1,0:T(8,128)} copy(f32[1,2,16,384]{3,2,1,0:T(8,128)} %get-tuple-element.6) | data formatting | bytes 98304
  40.3 0.0 copy-done.1
  40.3 0.0 copy-start
  40.3 0.6 %copy.19 = f32[1,2,16,128]{3,2,1,0:T(8,128)} copy(f32[1,2,16,128]{3,2,1,0:T(8,128)S(1)} %copy-done.1) | data formatting | bytes 32768
  40.9 0.1 copy-done
  41.0 0.6 %copy.20 = f32[1,2,16,128]{3,2,1,0:T(8,128)} copy(f32[1,2,16,128]{3,2,1,0:T(8,128)S(1)} %copy-done) | data formatting | bytes 32768
Async XLA Ops:
  38.9 1.4 %copy-start.1 = (f32[1,2,16,128]{3,2,1,0:T(8,128)S(1)}, f32[1,2,16,128]{3,2,1,0:T(8,128)}, u32[]{:S(2)}) copy-start(f32[1,2,16,128]{3,2,1,0:T(8,128)} %get-tuple-element.7) | copy-start | bytes 49156
  40.3 0.7 %copy-start = (f32[1,2,16,128]{3,2,1,0:T(8,128)S(1)}, f32[1,2,16,128]{3,2,1,0:T(8,128)}, u32[]{:S(2)}) copy-start(f32[1,2,16,128]{3,2,1,0:T(8,128)} %get-tuple-element.8) | copy-start | bytes 49156

commit v3 on v2

--- a/solution.py
+++ b/solution.py
@@ -9,6 +9,7 @@
 
 STEP = 16
 NNB = 3
+CHUNKS = 4
 
 highest = lax.Precision.HIGHEST
 
@@ -21,6 +22,16 @@
     return lax.dot_general(
         left, right, (((1,), (1,)), ((), ())), precision=highest, preferred_element_type=jnp.float32
     )
+
+
+def picked(rows, selection):
+    high = rows.astype(jnp.bfloat16).astype(jnp.float32)
+    middle = (rows - high).astype(jnp.bfloat16).astype(jnp.float32)
+    low = (rows - high) - middle
+    count = rows.shape[0]
+    parts = jnp.concatenate([high, middle, low, jnp.zeros_like(low)], axis=0)
+    out = jnp.dot(parts.astype(jnp.bfloat16), selection, preferred_element_type=jnp.float32)
+    return (out[0:count] + out[count : 2 * count]) + out[2 * count : 3 * count]
 
 
 def kernel(
@@ -73,6 +84,8 @@
     state_in,
     boundary_buf,
     boundary_in,
+    agreed_buf,
+    agreed_in,
     fetch_sem,
     coef_send,
     pass_send,
@@ -89,6 +102,8 @@
     state_recv,
     boundary_send,
     boundary_recv,
+    agreed_send,
+    agreed_recv,
 ):
     place = lax.axis_index("hor")
     share = lax.axis_index("scen")
@@ -222,9 +237,29 @@
     def state_copy(other):
         return copy_to("hor", place, other, state_buf.at[other], state_in, state_send, state_recv)
 
-    def boundary_copy(other):
+    def boundary_copy(chunk, other):
+        return pltpu.make_async_remote_copy(
+            src_ref=boundary_buf.at[chunk],
+            dst_ref=boundary_in.at[chunk, area],
+            send_sem=boundary_send.at[chunk, other],
+            recv_sem=boundary_recv.at[chunk, area],
+            device_id={"area": other},
+            device_id_type=pl.DeviceIdType.MESH,
+        )
+
+    def boundary_arrived(chunk, other):
+        pltpu.make_async_remote_copy(
+            src_ref=boundary_buf.at[chunk],
+            dst_ref=boundary_in.at[chunk, other],
+            send_sem=boundary_send.at[chunk, other],
+            recv_sem=boundary_recv.at[chunk, other],
+            device_id={"area": other},
+            device_id_type=pl.DeviceIdType.MESH,
+        ).wait_recv()
+
+    def agreed_copy(other):
         return copy_to(
-            "area", area, other, boundary_buf, boundary_in, boundary_send, boundary_recv
+            "hor", place, other, agreed_buf.at[other], agreed_in, agreed_send, agreed_recv
         )
 
     def arrived(axis, other, source, target, send, recv):
@@ -313,6 +348,7 @@
     def ahead_step(h, state):
         for j in (0, 1):
             state_buf[h, pl.ds(j, 1), :] = state[0:1, :]
+            costate_buf[pl.ds(2 * h + j, 1), :] = state[0:1, :]
             diag, up, down = (
                 wide(coef_in[h, c, pl.ds(j, 1), :]) for c in range(3)
             )
@@ -329,8 +365,39 @@
 
         return state
 
-    lax.fori_loop(0, segments, ahead_step, wide(start_ref[...]))
+    narrow = selection.astype(jnp.bfloat16)
+    chunks = boundary_buf.shape[0]
+    span = segments // chunks
+    state = wide(start_ref[...])
+    for chunk in range(chunks):
+        state = lax.fori_loop(chunk * span, (chunk + 1) * span, ahead_step, state)
+        boundary_buf[chunk] = picked(
+            costate_buf[pl.ds(2 * span * chunk, 2 * span), :], narrow
+        )
+        each(areas, area, lambda o, chunk=chunk: boundary_copy(chunk, o).start())
     state_in[place] = state_buf[place]
+
+    weights = []
+    for n in range(areas):
+        weight = jnp.where(area == n, 1.0, 0.0)
+        for j in range(NNB):
+            weight = weight + jnp.where(adjacency_ref[0, j] == n, 1.0, 0.0)
+        weights.append(weight * (1.0 / (NNB + 1)))
+    for chunk in range(chunks):
+        boundary_in[chunk, area] = boundary_buf[chunk]
+        each(areas, area, lambda o, chunk=chunk: boundary_arrived(chunk, o))
+        agreed = weights[0] * boundary_in[chunk, 0]
+        for n in range(1, areas):
+            agreed = agreed + weights[n] * boundary_in[chunk, n]
+        for i in range(span):
+            h = chunk * span + i
+            agreed_buf[h] = agreed[2 * i : 2 * i + 2, :]
+
+            @pl.when(h != place)
+            def _(h=h):
+                agreed_copy(h).start()
+
+    agreed_in[place] = agreed_buf[place]
     each(
         segments,
         place,
@@ -341,24 +408,17 @@
             trajectory_ref[0, t, pl.ds(s, 1), :] = state_in[s, pl.ds(t, 1), :]
     put_state = pltpu.make_async_copy(trajectory_ref, trajectory_hbm, fetch_sem.at[0])
     put_state.start()
+    own = [dual_ref[0, t] + picked(trajectory_ref[0, t], narrow) for t in range(2)]
+    each(
+        segments,
+        place,
+        lambda o: arrived("hor", o, agreed_buf.at[o], agreed_in, agreed_send, agreed_recv),
+    )
+    for s in range(scens):
+        for t in range(2):
+            agreed_ref[0, t, pl.ds(s, 1), :] = agreed_in[s, pl.ds(t, 1), :]
     for t in range(2):
-        boundary_buf[t] = product(trajectory_ref[0, t], selection)
-    each(areas, area, lambda o: boundary_copy(o).start())
-    boundary_in[area] = boundary_buf[...]
-    each(
-        areas,
-        area,
-        lambda o: arrived("area", o, boundary_buf, boundary_in, boundary_send, boundary_recv),
-    )
-    summed = boundary_buf[...]
-    for n in range(areas):
-        weight = jnp.float32(0.0)
-        for j in range(NNB):
-            weight = weight + jnp.where(adjacency_ref[0, j] == n, 1.0, 0.0)
-        summed = summed + weight * boundary_in[n]
-    agreed = summed * (1.0 / (NNB + 1))
-    agreed_ref[0] = agreed
-    updated_ref[0] = dual_ref[0] + boundary_buf[...] - agreed
+        updated_ref[0, t] = own[t] - agreed_ref[0, t]
     put_agreed = pltpu.make_async_copy(agreed_ref, agreed_hbm, fetch_sem.at[1])
     put_updated = pltpu.make_async_copy(updated_ref, updated_hbm, fetch_sem.at[2])
     put_agreed.start()
@@ -378,9 +438,11 @@
         mean_copy(o).wait_send()
         noise_copy(o).wait_send()
         state_copy(o).wait_send()
+        agreed_copy(o).wait_send()
 
     each(segments, place, drain)
-    each(areas, area, lambda o: boundary_copy(o).wait_send())
+    for chunk in range(chunks):
+        each(areas, area, lambda o, chunk=chunk: boundary_copy(chunk, o).wait_send())
     put_state.wait()
     put_agreed.wait()
     put_updated.wait()
@@ -404,6 +466,7 @@
     sharers = lax.axis_size("scen")
     areas = lax.axis_size("area")
     extent = diagonal.shape[-1]
+    shared_count = dual_values.shape[-1]
     anywhere = pl.BlockSpec(memory_space=pl.ANY)
     real = jnp.float32
     scratch = [
@@ -443,13 +506,17 @@
         pltpu.VMEM((2 * segments, extent), real),
         pltpu.VMEM((segments, 2, extent), real),
         pltpu.VMEM((segments, 2, extent), real),
-        pltpu.VMEM(dual_values.shape[1:], real),
-        pltpu.VMEM((areas, *dual_values.shape[1:]), real),
+        pltpu.VMEM((CHUNKS, 2 * segments // CHUNKS, shared_count), real),
+        pltpu.VMEM((CHUNKS, areas, 2 * segments // CHUNKS, shared_count), real),
+        pltpu.VMEM((segments, 2, shared_count), real),
+        pltpu.VMEM((segments, 2, shared_count), real),
     ]
     scratch += [pltpu.SemaphoreType.DMA((12,))]
     scratch += [pltpu.SemaphoreType.DMA((segments,)) for _ in range(3)]
-    for count in (segments, segments, sharers, segments, segments, areas):
+    for count in (segments, segments, sharers, segments, segments):
         scratch += [pltpu.SemaphoreType.DMA((count,)), pltpu.SemaphoreType.DMA((count,))]
+    scratch += [pltpu.SemaphoreType.DMA((CHUNKS, areas)) for _ in range(2)]
+    scratch += [pltpu.SemaphoreType.DMA((segments,)) for _ in range(2)]
     return pl.pallas_call(
         functools.partial(kernel, segments, sharers, areas),
         out_shape=(

time: 41.9 us -> 42.1 us (level)
  no operation moved by 1% of the time
where the time goes in v3:
time: 42.1 us; the launch traced here: 41.9 us
  Pallas kernels  38.5 us (91%)
  local copies, waits for them, and re-layouts  2.76 us (7%)
  between operations  0.65 us (2%)
    pallas_call x1, Pallas kernels, per_device(): pl.pallas_call(functools.partial(kernel, segments, sharers, areas), out_s...  38.5 us
    unnamed x7, local copies, waits for them, and re-layouts  2.76 us

profile of v3, /device:TPU:1, one launch (start us, length us, event | category | flops | bytes accessed | tf_op | source)
XLA Modules:
  0.0 41.9 jit_solution(11470750822576515803)
XLA Ops:
  0.6 38.5 %shard_map.139 = (f32[1,2,16,384]{3,2,1,0:T(8,128)}, f32[1,2,16,128]{3,2,1,0:T(8,128)}, f32[1,2,16,128]{3,2,1,0:T(8,128)}) custom-call(s32[1,4]{1,0:T(1,128)} %offsets_hbm.1, s32[1,3]{1,0:T(1,128)} %adjacency_hbm.1, f32[1,2,384]{2,1,0:T(2,128)} %diagonal_hbm.1, f32[1,2,4,384]{3,2,1,0:T(4,128)} %band_hbm.1, s32[1,128]{1,0:T(1,128)} %index_hbm.1, ...), custom_call_target="tpu_custom_call" | custom-call | tf_op jit(solution)/shard_map/pallas_call | solution.py:520
  39.1 0.0 copy-start.1
  39.1 1.4 %copy.18 = f32[1,2,16,384]{3,2,1,0:T(8,128)} copy(f32[1,2,16,384]{3,2,1,0:T(8,128)} %get-tuple-element.6) | data formatting | bytes 98304
  40.5 0.0 copy-done.1
  40.5 0.0 copy-start
  40.5 0.6 %copy.19 = f32[1,2,16,128]{3,2,1,0:T(8,128)} copy(f32[1,2,16,128]{3,2,1,0:T(8,128)S(1)} %copy-done.1) | data formatting | bytes 32768
  41.1 0.1 copy-done
  41.3 0.6 %copy.20 = f32[1,2,16,128]{3,2,1,0:T(8,128)} copy(f32[1,2,16,128]{3,2,1,0:T(8,128)S(1)} %copy-done) | data formatting | bytes 32768
Async XLA Ops:
  39.1 1.4 %copy-start.1 = (f32[1,2,16,128]{3,2,1,0:T(8,128)S(1)}, f32[1,2,16,128]{3,2,1,0:T(8,128)}, u32[]{:S(2)}) copy-start(f32[1,2,16,128]{3,2,1,0:T(8,128)} %get-tuple-element.7) | copy-start | bytes 49156
  40.5 0.7 %copy-start = (f32[1,2,16,128]{3,2,1,0:T(8,128)S(1)}, f32[1,2,16,128]{3,2,1,0:T(8,128)}, u32[]{:S(2)}) copy-start(f32[1,2,16,128]{3,2,1,0:T(8,128)} %get-tuple-element.8) | copy-start | bytes 49156

commit v4 on v2

--- a/solution.py
+++ b/solution.py
@@ -23,12 +23,44 @@
     )
 
 
+def in_parts(rows):
+    high = rows.astype(jnp.bfloat16).astype(jnp.float32)
+    middle = (rows - high).astype(jnp.bfloat16).astype(jnp.float32)
+    return high, middle, (rows - high) - middle
+
+
+def picked(rows, selection):
+    count = rows.shape[0]
+    parts = list(in_parts(rows))
+    if 3 * count % 16:
+        parts.append(jnp.zeros((16 - 3 * count % 16, rows.shape[1]), jnp.float32))
+    parts = jnp.concatenate(parts, axis=0).astype(jnp.bfloat16)
+    out = jnp.dot(parts, selection, preferred_element_type=jnp.float32)
+    return (out[0:count] + out[count : 2 * count]) + out[2 * count : 3 * count]
+
+
+def finish(
+    adjacency_ref, dual_ref, state_ref, boundary_ref, trajectory_ref, agreed_ref, updated_ref
+):
+    area = lax.axis_index("area")
+    own = boundary_ref[area]
+    summed = own
+    for n in range(boundary_ref.shape[0]):
+        weight = jnp.float32(0.0)
+        for j in range(NNB):
+            weight = weight + jnp.where(adjacency_ref[0, j] == n, 1.0, 0.0)
+        summed = summed + weight * boundary_ref[n]
+    agreed = summed * (1.0 / (NNB + 1))
+    trajectory_ref[...] = state_ref[...]
+    agreed_ref[0] = agreed
+    updated_ref[0] = dual_ref[0] + own - agreed
+
+
 def kernel(
     segments,
     sharers,
     areas,
     offsets_hbm,
-    adjacency_hbm,
     diagonal_hbm,
     band_hbm,
     index_hbm,
@@ -40,10 +72,8 @@
     consensus_hbm,
     dual_hbm,
     trajectory_hbm,
-    agreed_hbm,
-    updated_hbm,
+    boundary_in,
     offsets_ref,
-    adjacency_ref,
     diagonal_ref,
     band_ref,
     index_ref,
@@ -55,8 +85,6 @@
     consensus_ref,
     dual_ref,
     trajectory_ref,
-    agreed_ref,
-    updated_ref,
     grad_buf,
     coef_in,
     pack_buf,
@@ -72,7 +100,7 @@
     state_buf,
     state_in,
     boundary_buf,
-    boundary_in,
+    matrix_buf,
     fetch_sem,
     coef_send,
     pass_send,
@@ -129,7 +157,6 @@
                 (matrix_hbm, matrix_ref),
                 (penalty_hbm, penalty_ref),
                 (start_hbm, start_ref),
-                (adjacency_hbm, adjacency_ref),
             )
         )
     ]
@@ -169,6 +196,13 @@
     noise_in[place] = noise_buf[place]
     part_in[share] = part_buf[...]
 
+    for fetch in fetches[8:]:
+        fetch.wait()
+    inputs = matrix_ref.shape[-1]
+    matrix_high, matrix_low, _ = in_parts(matrix_ref[0])
+    matrix_buf[:, 0:inputs] = matrix_high.astype(jnp.bfloat16)
+    matrix_buf[:, inputs : 2 * inputs] = matrix_low.astype(jnp.bfloat16)
+
     pl.semaphore_wait(barrier, segments + sharers + areas - 3)
 
     def copy_to(axis, own, other, source, target, send, recv):
@@ -296,14 +330,23 @@
 
     lax.fori_loop(0, segments, back, jnp.zeros((8, extent), jnp.float32))
 
-    for fetch in fetches[8:]:
-        fetch.wait()
-    controls = -product(costate_buf[...], matrix_ref[0]) / penalty_ref[...]
+    matrix_parts = matrix_buf[...]
+    spread = picked(costate_buf[...], matrix_parts)
+    controls = spread[:, 0:inputs] + spread[:, inputs : 2 * inputs]
+    controls = -controls / penalty_ref[...]
     shared = controls[2 * segments + 1 : 2 * segments + 2, :]
     controls = controls[0 : 2 * segments, :]
     at_start = lax.broadcasted_iota(jnp.int32, controls.shape, 0) == 0
     controls = jnp.where(at_start, jnp.broadcast_to(shared, controls.shape), controls)
-    force_buf[...] = product_transposed(controls, matrix_ref[0])
+    count = 2 * segments
+    parts = jnp.concatenate(in_parts(controls), axis=0).astype(jnp.bfloat16)
+    force = lax.dot_general(
+        jnp.concatenate([parts, parts], axis=1),
+        matrix_parts,
+        (((1,), (1,)), ((), ())),
+        preferred_element_type=jnp.float32,
+    )
+    force_buf[...] = (force[0:count] + force[count : 2 * count]) + force[2 * count : 3 * count]
     each(
         segments,
         place,
@@ -341,28 +384,12 @@
             trajectory_ref[0, t, pl.ds(s, 1), :] = state_in[s, pl.ds(t, 1), :]
     put_state = pltpu.make_async_copy(trajectory_ref, trajectory_hbm, fetch_sem.at[0])
     put_state.start()
+    narrow = selection.astype(jnp.bfloat16)
     for t in range(2):
-        boundary_buf[t] = product(trajectory_ref[0, t], selection)
+        boundary_buf[t] = picked(trajectory_ref[0, t], narrow)
     each(areas, area, lambda o: boundary_copy(o).start())
-    boundary_in[area] = boundary_buf[...]
-    each(
-        areas,
-        area,
-        lambda o: arrived("area", o, boundary_buf, boundary_in, boundary_send, boundary_recv),
-    )
-    summed = boundary_buf[...]
-    for n in range(areas):
-        weight = jnp.float32(0.0)
-        for j in range(NNB):
-            weight = weight + jnp.where(adjacency_ref[0, j] == n, 1.0, 0.0)
-        summed = summed + weight * boundary_in[n]
-    agreed = summed * (1.0 / (NNB + 1))
-    agreed_ref[0] = agreed
-    updated_ref[0] = dual_ref[0] + boundary_buf[...] - agreed
-    put_agreed = pltpu.make_async_copy(agreed_ref, agreed_hbm, fetch_sem.at[1])
-    put_updated = pltpu.make_async_copy(updated_ref, updated_hbm, fetch_sem.at[2])
-    put_agreed.start()
-    put_updated.start()
+    put_boundary = pltpu.make_async_copy(boundary_buf, boundary_in.at[area], fetch_sem.at[1])
+    put_boundary.start()
 
     each(sharers, share, lambda o: part_copy(o).wait_send())
 
@@ -382,8 +409,12 @@
     each(segments, place, drain)
     each(areas, area, lambda o: boundary_copy(o).wait_send())
     put_state.wait()
-    put_agreed.wait()
-    put_updated.wait()
+    put_boundary.wait()
+    each(
+        areas,
+        area,
+        lambda o: arrived("area", o, boundary_buf, boundary_in, boundary_send, boundary_recv),
+    )
 
 
 def per_device(
@@ -408,7 +439,6 @@
     real = jnp.float32
     scratch = [
         pltpu.SMEM(band_offsets.shape, jnp.int32),
-        pltpu.SMEM(adjacency.shape, jnp.int32),
     ]
     scratch += [
         pltpu.VMEM(held.shape, held.dtype)
@@ -424,8 +454,6 @@
             consensus,
             dual_values,
             linear_cost,
-            dual_values,
-            dual_values,
         )
     ]
     scratch += [
@@ -444,26 +472,24 @@
         pltpu.VMEM((segments, 2, extent), real),
         pltpu.VMEM((segments, 2, extent), real),
         pltpu.VMEM(dual_values.shape[1:], real),
-        pltpu.VMEM((areas, *dual_values.shape[1:]), real),
+        pltpu.VMEM((extent, 2 * input_matrix.shape[-1]), jnp.bfloat16),
     ]
     scratch += [pltpu.SemaphoreType.DMA((12,))]
     scratch += [pltpu.SemaphoreType.DMA((segments,)) for _ in range(3)]
     for count in (segments, segments, sharers, segments, segments, areas):
         scratch += [pltpu.SemaphoreType.DMA((count,)), pltpu.SemaphoreType.DMA((count,))]
-    return pl.pallas_call(
+    states, boundaries = pl.pallas_call(
         functools.partial(kernel, segments, sharers, areas),
         out_shape=(
             jax.ShapeDtypeStruct(linear_cost.shape, real),
-            jax.ShapeDtypeStruct(dual_values.shape, real),
-            jax.ShapeDtypeStruct(dual_values.shape, real),
+            jax.ShapeDtypeStruct((areas, *dual_values.shape[1:]), real),
         ),
-        in_specs=[anywhere] * 12,
-        out_specs=(anywhere,) * 3,
+        in_specs=[anywhere] * 11,
+        out_specs=(anywhere,) * 2,
         scratch_shapes=scratch,
         compiler_params=pltpu.CompilerParams(collective_id=0, has_side_effects=True),
     )(
         band_offsets,
-        adjacency,
         diagonal,
         band_coef,
         boundary_index,
@@ -475,6 +501,17 @@
         consensus,
         dual_values,
     )
+    vmem = pl.BlockSpec(memory_space=pltpu.VMEM)
+    return pl.pallas_call(
+        finish,
+        out_shape=(
+            jax.ShapeDtypeStruct(linear_cost.shape, real),
+            jax.ShapeDtypeStruct(dual_values.shape, real),
+            jax.ShapeDtypeStruct(dual_values.shape, real),
+        ),
+        in_specs=[pl.BlockSpec(memory_space=pltpu.SMEM)] + [vmem] * 3,
+        out_specs=(vmem,) * 3,
+    )(adjacency, dual_values, states, boundaries)
 
 
 def solution(mesh):

time: 41.9 us -> 39.7 us (0.947)
  local copies, waits for them, and re-layouts: 2.76 us -> 0 us
  Pallas kernels: 38.2 us -> 38.9 us
    unnamed x7 -> x0, local copies, waits for them, and re-layouts: 2.76 us -> none
    pallas_call x0 -> x1, Pallas kernels: none -> 1.62 us  [per_device(): pl.pallas_call(finish, out_shape=(jax.ShapeDtypeStruct(linear_cost.shape,...]
    pallas_call x1, Pallas kernels: 38.2 us -> 37.3 us  [per_device(): pl.pallas_call(functools.partial(kernel, segments, sharers, areas), out_s...]
where the time goes in v4:
time: 39.7 us; the launch traced here: 39.6 us
  Pallas kernels  38.9 us (98%)
  between operations  0.64 us (2%)
    pallas_call x1, Pallas kernels, per_device(): pl.pallas_call(functools.partial(kernel, segments, sharers, areas), out_s...  37.3 us
    pallas_call x1, Pallas kernels, per_device(): pl.pallas_call(finish, out_shape=(jax.ShapeDtypeStruct(linear_cost.shape,...  1.62 us

profile of v4, /device:TPU:1, one launch (start us, length us, event | category | flops | bytes accessed | tf_op | source)
XLA Modules:
  0.0 39.6 jit_solution(14614029679975042671)
XLA Ops:
  0.6 37.3 %shard_map.139 = (f32[1,2,16,384]{3,2,1,0:T(8,128)}, f32[8,2,16,128]{3,2,1,0:T(8,128)}) custom-call(s32[1,4]{1,0:T(1,128)} %offsets_hbm.1, f32[1,2,384]{2,1,0:T(2,128)} %diagonal_hbm.1, f32[1,2,4,384]{3,2,1,0:T(4,128)} %band_hbm.1, s32[1,128]{1,0:T(1,128)} %index_hbm.1, f32[1,384]{1,0:T(1,128)} %start_hbm.1, f32[1,384,128]{2,1,0:T(8,128)} %matrix_hbm.1, ...), custom_call_target="tpu_custom_call" | custom-call | tf_op jit(solution)/shard_map/pallas_call | solution.py:481
  38.0 1.6 %shard_map.140 = (f32[1,2,16,384]{3,2,1,0:T(8,128)}, f32[1,2,16,128]{3,2,1,0:T(8,128)}, f32[1,2,16,128]{3,2,1,0:T(8,128)}) custom-call(s32[1,3]{1,0:T(1,128)} %adjacency_ref.1, f32[1,2,16,128]{3,2,1,0:T(8,128)} %dual_ref.1, f32[1,2,16,384]{3,2,1,0:T(8,128)} %get-tuple-element.5.state_ref, f32[8,2,16,128]{3,2,1,0:T(8,128)} %get-tuple-element.6.boundary_ref), custom_call_target="tpu_custom_call" | custom-call | tf_op jit(solution)/shard_map/pallas_call | solution.py:505

commit v5 on v4

--- a/solution.py
+++ b/solution.py
@@ -256,9 +256,14 @@
     def state_copy(other):
         return copy_to("hor", place, other, state_buf.at[other], state_in, state_send, state_recv)
 
-    def boundary_copy(other):
-        return copy_to(
-            "area", area, other, boundary_buf, boundary_in, boundary_send, boundary_recv
+    def boundary_copy(t, other, own):
+        return pltpu.make_async_remote_copy(
+            src_ref=boundary_buf.at[t],
+            dst_ref=boundary_in.at[own, t],
+            send_sem=boundary_send.at[t, other],
+            recv_sem=boundary_recv.at[t, own],
+            device_id={"area": other},
+            device_id_type=pl.DeviceIdType.MESH,
         )
 
     def arrived(axis, other, source, target, send, recv):
@@ -374,12 +379,12 @@
 
     lax.fori_loop(0, segments, ahead_step, wide(start_ref[...]))
     state_in[place] = state_buf[place]
-    each(
-        segments,
-        place,
-        lambda o: arrived("hor", o, state_buf.at[o], state_in, state_send, state_recv),
-    )
     for s in range(scens):
+
+        @pl.when(s != place)
+        def _(s=s):
+            arrived("hor", s, state_buf.at[s], state_in, state_send, state_recv)
+
         for t in range(2):
             trajectory_ref[0, t, pl.ds(s, 1), :] = state_in[s, pl.ds(t, 1), :]
     put_state = pltpu.make_async_copy(trajectory_ref, trajectory_hbm, fetch_sem.at[0])
@@ -387,7 +392,7 @@
     narrow = selection.astype(jnp.bfloat16)
     for t in range(2):
         boundary_buf[t] = picked(trajectory_ref[0, t], narrow)
-    each(areas, area, lambda o: boundary_copy(o).start())
+        each(areas, area, lambda o, t=t: boundary_copy(t, o, area).start())
     put_boundary = pltpu.make_async_copy(boundary_buf, boundary_in.at[area], fetch_sem.at[1])
     put_boundary.start()
 
@@ -407,14 +412,12 @@
         state_copy(o).wait_send()
 
     each(segments, place, drain)
-    each(areas, area, lambda o: boundary_copy(o).wait_send())
+    for t in range(2):
+        each(areas, area, lambda o, t=t: boundary_copy(t, o, area).wait_send())
     put_state.wait()
     put_boundary.wait()
-    each(
-        areas,
-        area,
-        lambda o: arrived("area", o, boundary_buf, boundary_in, boundary_send, boundary_recv),
-    )
+    for t in range(2):
+        each(areas, area, lambda o, t=t: boundary_copy(t, o, o).wait_recv())
 
 
 def per_device(
@@ -476,8 +479,9 @@
     ]
     scratch += [pltpu.SemaphoreType.DMA((12,))]
     scratch += [pltpu.SemaphoreType.DMA((segments,)) for _ in range(3)]
-    for count in (segments, segments, sharers, segments, segments, areas):
+    for count in (segments, segments, sharers, segments, segments):
         scratch += [pltpu.SemaphoreType.DMA((count,)), pltpu.SemaphoreType.DMA((count,))]
+    scratch += [pltpu.SemaphoreType.DMA((2, areas)) for _ in range(2)]
     states, boundaries = pl.pallas_call(
         functools.partial(kernel, segments, sharers, areas),
         out_shape=(

time: 39.7 us -> 39.9 us (level)
  no operation moved by 1% of the time
where the time goes in v5:
time: 39.9 us; the launch traced here: 39.7 us
  Pallas kernels  39.1 us (98%)
  between operations  0.64 us (2%)
    pallas_call x1, Pallas kernels, per_device(): pl.pallas_call(functools.partial(kernel, segments, sharers, areas), out_s...  37.5 us
    pallas_call x1, Pallas kernels, per_device(): pl.pallas_call(finish, out_shape=(jax.ShapeDtypeStruct(linear_cost.shape,...  1.62 us

profile of v5, /device:TPU:1, one launch (start us, length us, event | category | flops | bytes accessed | tf_op | source)
XLA Modules:
  0.0 39.7 jit_solution(13369360740405713514)
XLA Ops:
  0.6 37.5 %shard_map.139 = (f32[1,2,16,384]{3,2,1,0:T(8,128)}, f32[8,2,16,128]{3,2,1,0:T(8,128)}) custom-call(s32[1,4]{1,0:T(1,128)} %offsets_hbm.1, f32[1,2,384]{2,1,0:T(2,128)} %diagonal_hbm.1, f32[1,2,4,384]{3,2,1,0:T(4,128)} %band_hbm.1, s32[1,128]{1,0:T(1,128)} %index_hbm.1, f32[1,384]{1,0:T(1,128)} %start_hbm.1, f32[1,384,128]{2,1,0:T(8,128)} %matrix_hbm.1, ...), custom_call_target="tpu_custom_call" | custom-call | tf_op jit(solution)/shard_map/pallas_call | solution.py:485
  38.1 1.6 %shard_map.140 = (f32[1,2,16,384]{3,2,1,0:T(8,128)}, f32[1,2,16,128]{3,2,1,0:T(8,128)}, f32[1,2,16,128]{3,2,1,0:T(8,128)}) custom-call(s32[1,3]{1,0:T(1,128)} %adjacency_ref.1, f32[1,2,16,128]{3,2,1,0:T(8,128)} %dual_ref.1, f32[1,2,16,384]{3,2,1,0:T(8,128)} %get-tuple-element.5.state_ref, f32[8,2,16,128]{3,2,1,0:T(8,128)} %get-tuple-element.6.boundary_ref), custom_call_target="tpu_custom_call" | custom-call | tf_op jit(solution)/shard_map/pallas_call | solution.py:509
